TPU v7x, 128 devices: a whole 4x4x4 slice. The times are simulated.
128 devices in a mesh: blk: 16 (over x_hi, y, core), bal: 8 (over x_lo, z).
Axes of the slice: x: 4 (x_hi: 2, x_lo: 2; x = x_hi * 2 + x_lo), y: 4, z: 4, core: 2. Of those that a mesh axis runs over, the one named last changes fastest.
Arguments:
- features: bfloat16 [131072, 512], P('blk', 'bal'), may hold values from -6 to 6
- tile_values: bfloat16 [16, 16, 32, 128, 128], P('blk'), may hold values from 0.049804688 to 1
- tile_rows: int32 [16, 16, 32], P('blk'), may hold values from 0 to 63
- tile_cols: int32 [16, 16, 32], P('blk'), may hold values from 0 to 63
- tile_counts: int32 [16, 16], P('blk'), may hold values from 8 to 32, as said below
- w_self: bfloat16 [512, 512], replicated, may hold values from -0.25 to 0.25
- w_neigh: bfloat16 [512, 512], replicated, may hold values from -6 to 6
- bias: float32 [512], replicated, may hold values from -3 to 3
- part_map: int32 [16, 64], P('blk'), may hold values from 0 to 7, as said below
Outputs:
- next_rows: bfloat16 [16, 8, 2048, 512], P('blk', 'bal')
Inputs may be any that keep to these rules, and one draw needn't show every extreme that they name: `tile_counts`: live slots of one pair of vertex blocks; the most, 32, is reached by some pair in every draw. `part_map`: within one block of vertex rows at most 16 tiles go to any one value, and exactly 16 to some value.
All inputs are finite; a program needn't handle non-finite values.
Results may differ from a plain program's by a relative error of at most 0.0036.
Values may be sent and summed in bfloat16 or wider, within the bound.
No kernel may reach another device: no remote copies, remote signals or barrier semaphores. Data moves between devices by JAX's collectives and lax.ppermute only.
A program may use at most 128 MiB of HBM per device.

v0:
```python
import jax
import jax.numpy as jnp
from jax import lax
from jax.sharding import PartitionSpec as P

TILE = 128


def from_behind(block, axis, distance):
    devices = range(lax.axis_size(axis))
    route = [((i - distance) % len(devices), i) for i in devices]
    return lax.ppermute(block, axis, route)


def advance(block, steps_by):
    return from_behind(block, "blk", steps_by)


def on_device(
    features, tile_values, tile_rows, tile_cols, tile_counts, w_self, w_neigh, bias, part_map
):
    n_blk = lax.axis_size("blk")
    n_bal = lax.axis_size("bal")
    here = lax.axis_index("blk")
    column = lax.axis_index("bal")
    width = features.shape[1]
    tiles_per = part_map.shape[1]
    values = tile_values[0]
    rows_idx = tile_rows[0]
    cols_idx = tile_cols[0]
    counts = tile_counts[0]
    slots = values.shape[1]
    live = jnp.arange(slots)[None, :] < counts[:, None]
    row_hot = (
        (rows_idx[:, :, None] == jnp.arange(tiles_per)[None, None, :]) & live[:, :, None]
    ).astype(jnp.float32)
    row_mass = jnp.einsum(
        "csij,j->csi", values, jnp.ones((TILE,), jnp.bfloat16), preferred_element_type=jnp.float32
    )
    degree = 1.0 + jnp.einsum("cst,csi->ti", row_hot, row_mass, precision=lax.Precision.HIGHEST)

    def absorb(total, block, source):
        tiles = block.reshape(tiles_per, TILE, width)
        vals = lax.dynamic_index_in_dim(values, source, 0, keepdims=False)
        picks = lax.dynamic_index_in_dim(cols_idx, source, 0, keepdims=False)
        targets = lax.dynamic_index_in_dim(rows_idx, source, 0, keepdims=False)
        alive = lax.dynamic_index_in_dim(live, source, 0, keepdims=False)
        gathered = jnp.take(tiles, picks, axis=0)
        prod = jnp.einsum("sij,sjf->sif", vals, gathered, preferred_element_type=jnp.float32)
        masked = jnp.where(alive[:, None, None], prod, 0.0)
        return total.at[targets].add(masked)

    empty = jnp.zeros((tiles_per, TILE, width), jnp.float32)

    def step_one(index, carry):
        total, block = carry
        total = absorb(total, block, (here - index) % n_blk)
        block = advance(block, 1)
        return (total, block)

    total, block = lax.fori_loop(0, n_blk - 1, step_one, (empty, features))
    total = absorb(total, block, (here - (n_blk - 1)) % n_blk)
    mean_agg = (total / degree[:, :, None]).astype(jnp.bfloat16).reshape(tiles_per * TILE, width)
    capacity = 2 * tiles_per // n_bal
    mapping = part_map[0]
    dest_hot = (mapping[:, None] == jnp.arange(n_bal)[None, :]).astype(jnp.int32)
    ranks = jnp.cumsum(dest_hot, axis=0) - dest_hot
    place = mapping * capacity + jnp.sum(ranks * dest_hot, axis=1)
    select = (jnp.arange(n_bal * capacity)[:, None] == place[None, :]).astype(jnp.bfloat16)
    col_start = column * width
    zeros_out = jnp.zeros((tiles_per * TILE, width), jnp.float32)
    carry = zeros_out
    mean_piece = lax.all_gather(mean_agg, "bal", axis=1, tiled=True)
    feat_piece = lax.all_gather(features, "bal", axis=1, tiled=True)
    count = mean_piece.shape[1]
    neigh_part = lax.dynamic_slice(w_neigh, (0, col_start), (count, width))
    self_part = lax.dynamic_slice(w_self, (0, col_start), (count, width))
    carry = jnp.dot(mean_piece, neigh_part, preferred_element_type=jnp.float32)
    pre = carry + jnp.dot(feat_piece, self_part, preferred_element_type=jnp.float32)
    pre = pre + lax.dynamic_slice_in_dim(bias, col_start, width)
    hidden = jnp.maximum(pre, 0.0).astype(jnp.bfloat16)
    tiles = hidden.reshape(tiles_per, TILE, width)
    placed = jnp.einsum("kt,tif->kif", select, tiles, preferred_element_type=jnp.float32)
    result = lax.all_to_all(
        placed.astype(jnp.bfloat16).reshape(n_bal, capacity * TILE, width),
        "bal",
        split_axis=0,
        concat_axis=2,
        tiled=True,
    )
    return result[None]


def solution(mesh):
    placed = (
        P("blk", "bal"),
        P("blk", None, None, None, None),
        P("blk", None, None),
        P("blk", None, None),
        P("blk", None),
        P(),
        P(),
        P(),
        P("blk", None),
    )
    return jax.shard_map(
        on_device,
        mesh=mesh,
        in_specs=placed,
        out_specs=P("blk", "bal", None, None),
        check_vma=False,
    )
```

profile of v0, /device:TPU:0, one launch (start us, length us, event | category | flops | bytes accessed | tf_op | source)
XLA Modules:
  0.0 528.4 jit_solution(13366378268195812882)
XLA Ops:
  7.3 2.3 copy.33
  10.5 1.6 broadcast_in_dim.81
  12.0 343.1 %while.17 = (s32[]{:T(128)}, f32[64,128,64]{1,2,0:T(8,128)}, bf16[8192,64]{0,1:T(8,128)(2,1)}, s32[]{:T(128)}, s32[16,32]{1,0:T(8,128)S(1)}, /*index=5*/pred[16,...) while((s32[]{:T(128)}, f32[64,128,64]{1,2,0:T(8,128)}, ...), condition=%wide.region_4.6_spmd, body=%wide.region_2.5_spmd.sunk | while | flops 67896624 | bytes 15209832 | solution.py:61
  15.0 2.1 convolution_select_fusion.3
  17.0 4.9 scatter_fusion
  21.9 20.0 %collective-permute-done = bf16[8192,64]{0,1:T(8,128)(2,1)} collective-permute-done((bf16[8192,64]{0,1:T(8,128)(2,1)S(1)}, bf16[8192,64]{0,1:T(8,128)(2,1)}, u32[]{:S(2)}, u32[]{:S(2)}) %collective-permute-start) | collective-permute-done | bytes 1048608 | tf_op jit(solution)/shard_map/while/body/eval_jaxpr/ppermute | solution.py:12
  41.9 1.2 copy.36
  44.9 2.1 convolution_select_fusion.3
  47.0 4.8 scatter_fusion
  51.8 31.8 %collective-permute-done = bf16[8192,64]{0,1:T(8,128)(2,1)} collective-permute-done((bf16[8192,64]{0,1:T(8,128)(2,1)S(1)}, bf16[8192,64]{0,1:T(8,128)(2,1)}, u32[]{:S(2)}, u32[]{:S(2)}) %collective-permute-start) | collective-permute-done | bytes 1048608 | tf_op jit(solution)/shard_map/while/body/eval_jaxpr/ppermute | solution.py:12
  86.5 2.1 convolution_select_fusion.3
  88.5 4.8 scatter_fusion
  93.3 31.8 %collective-permute-done = bf16[8192,64]{0,1:T(8,128)(2,1)} collective-permute-done((bf16[8192,64]{0,1:T(8,128)(2,1)S(1)}, bf16[8192,64]{0,1:T(8,128)(2,1)}, u32[]{:S(2)}, u32[]{:S(2)}) %collective-permute-start) | collective-permute-done | bytes 1048608 | tf_op jit(solution)/shard_map/while/body/eval_jaxpr/ppermute | solution.py:12
  128.1 2.1 convolution_select_fusion.3
  130.2 4.8 scatter_fusion
  134.9 9.4 %collective-permute-done = bf16[8192,64]{0,1:T(8,128)(2,1)} collective-permute-done((bf16[8192,64]{0,1:T(8,128)(2,1)S(1)}, bf16[8192,64]{0,1:T(8,128)(2,1)}, u32[]{:S(2)}, u32[]{:S(2)}) %collective-permute-start) | collective-permute-done | bytes 1048608 | tf_op jit(solution)/shard_map/while/body/eval_jaxpr/ppermute | solution.py:12
  147.2 2.1 convolution_select_fusion.3
  149.3 4.8 scatter_fusion
  154.1 9.4 %collective-permute-done = bf16[8192,64]{0,1:T(8,128)(2,1)} collective-permute-done((bf16[8192,64]{0,1:T(8,128)(2,1)S(1)}, bf16[8192,64]{0,1:T(8,128)(2,1)}, u32[]{:S(2)}, u32[]{:S(2)}) %collective-permute-start) | collective-permute-done | bytes 1048608 | tf_op jit(solution)/shard_map/while/body/eval_jaxpr/ppermute | solution.py:12
  166.4 2.1 convolution_select_fusion.3
  168.5 4.8 scatter_fusion
  173.3 9.4 %collective-permute-done = bf16[8192,64]{0,1:T(8,128)(2,1)} collective-permute-done((bf16[8192,64]{0,1:T(8,128)(2,1)S(1)}, bf16[8192,64]{0,1:T(8,128)(2,1)}, u32[]{:S(2)}, u32[]{:S(2)}) %collective-permute-start) | collective-permute-done | bytes 1048608 | tf_op jit(solution)/shard_map/while/body/eval_jaxpr/ppermute | solution.py:12
  185.6 2.1 convolution_select_fusion.3
  187.7 4.8 scatter_fusion
  192.4 9.4 %collective-permute-done = bf16[8192,64]{0,1:T(8,128)(2,1)} collective-permute-done((bf16[8192,64]{0,1:T(8,128)(2,1)S(1)}, bf16[8192,64]{0,1:T(8,128)(2,1)}, u32[]{:S(2)}, u32[]{:S(2)}) %collective-permute-start) | collective-permute-done | bytes 1048608 | tf_op jit(solution)/shard_map/while/body/eval_jaxpr/ppermute | solution.py:12
  204.8 2.1 convolution_select_fusion.3
  206.8 4.8 scatter_fusion
  211.6 9.4 %collective-permute-done = bf16[8192,64]{0,1:T(8,128)(2,1)} collective-permute-done((bf16[8192,64]{0,1:T(8,128)(2,1)S(1)}, bf16[8192,64]{0,1:T(8,128)(2,1)}, u32[]{:S(2)}, u32[]{:S(2)}) %collective-permute-start) | collective-permute-done | bytes 1048608 | tf_op jit(solution)/shard_map/while/body/eval_jaxpr/ppermute | solution.py:12
  221.0 1.2 copy.36
  223.9 2.1 convolution_select_fusion.3
  226.0 4.8 scatter_fusion
  230.8 9.4 %collective-permute-done = bf16[8192,64]{0,1:T(8,128)(2,1)} collective-permute-done((bf16[8192,64]{0,1:T(8,128)(2,1)S(1)}, bf16[8192,64]{0,1:T(8,128)(2,1)}, u32[]{:S(2)}, u32[]{:S(2)}) %collective-permute-start) | collective-permute-done | bytes 1048608 | tf_op jit(solution)/shard_map/while/body/eval_jaxpr/ppermute | solution.py:12
  243.1 2.1 convolution_select_fusion.3
  245.2 4.8 scatter_fusion
  249.9 9.4 %collective-permute-done = bf16[8192,64]{0,1:T(8,128)(2,1)} collective-permute-done((bf16[8192,64]{0,1:T(8,128)(2,1)S(1)}, bf16[8192,64]{0,1:T(8,128)(2,1)}, u32[]{:S(2)}, u32[]{:S(2)}) %collective-permute-start) | collective-permute-done | bytes 1048608 | tf_op jit(solution)/shard_map/while/body/eval_jaxpr/ppermute | solution.py:12
  262.3 2.1 convolution_select_fusion.3
  264.3 4.8 scatter_fusion
  269.1 9.4 %collective-permute-done = bf16[8192,64]{0,1:T(8,128)(2,1)} collective-permute-done((bf16[8192,64]{0,1:T(8,128)(2,1)S(1)}, bf16[8192,64]{0,1:T(8,128)(2,1)}, u32[]{:S(2)}, u32[]{:S(2)}) %collective-permute-start) | collective-permute-done | bytes 1048608 | tf_op jit(solution)/shard_map/while/body/eval_jaxpr/ppermute | solution.py:12
  278.5 1.2 copy.36
  281.4 2.1 convolution_select_fusion.3
  283.5 4.8 scatter_fusion
  288.3 9.4 %collective-permute-done = bf16[8192,64]{0,1:T(8,128)(2,1)} collective-permute-done((bf16[8192,64]{0,1:T(8,128)(2,1)S(1)}, bf16[8192,64]{0,1:T(8,128)(2,1)}, u32[]{:S(2)}, u32[]{:S(2)}) %collective-permute-start) | collective-permute-done | bytes 1048608 | tf_op jit(solution)/shard_map/while/body/eval_jaxpr/ppermute | solution.py:12
  300.6 2.1 convolution_select_fusion.3
  302.7 4.8 scatter_fusion
  307.4 9.4 %collective-permute-done = bf16[8192,64]{0,1:T(8,128)(2,1)} collective-permute-done((bf16[8192,64]{0,1:T(8,128)(2,1)S(1)}, bf16[8192,64]{0,1:T(8,128)(2,1)}, u32[]{:S(2)}, u32[]{:S(2)}) %collective-permute-start) | collective-permute-done | bytes 1048608 | tf_op jit(solution)/shard_map/while/body/eval_jaxpr/ppermute | solution.py:12
  319.8 2.1 convolution_select_fusion.3
  321.8 4.8 scatter_fusion
  326.6 9.4 %collective-permute-done = bf16[8192,64]{0,1:T(8,128)(2,1)} collective-permute-done((bf16[8192,64]{0,1:T(8,128)(2,1)S(1)}, bf16[8192,64]{0,1:T(8,128)(2,1)}, u32[]{:S(2)}, u32[]{:S(2)}) %collective-permute-start) | collective-permute-done | bytes 1048608 | tf_op jit(solution)/shard_map/while/body/eval_jaxpr/ppermute | solution.py:12
  336.0 1.2 copy.36
  338.9 2.1 convolution_select_fusion.3
  341.0 4.8 scatter_fusion
  345.8 9.4 %collective-permute-done = bf16[8192,64]{0,1:T(8,128)(2,1)} collective-permute-done((bf16[8192,64]{0,1:T(8,128)(2,1)S(1)}, bf16[8192,64]{0,1:T(8,128)(2,1)}, u32[]{:S(2)}, u32[]{:S(2)}) %collective-permute-start) | collective-permute-done | bytes 1048608 | tf_op jit(solution)/shard_map/while/body/eval_jaxpr/ppermute | solution.py:12
  355.2 2.5 copy_bitcast_fusion.2
  357.7 2.0 gather_fusion.1
  359.7 3.1 convolution_select_fusion.1
  362.9 3.8 scatter_fusion.1
  366.6 10.2 %fusion.38 = f32[1,16,32,128]{3,0,2,1:T(1,128)S(1)} fusion(bf16[1,16,32,128,128]{4,3,2,1,0:T(8,128)(2,1)} %bitcast.106), kind=kOutput, calls=%fused_computation.70 | convolution fusion | flops 16777216 | bytes 17039360 | tf_op jit(solution)/shard_map/csij,j->csi/dot_general | solution.py:37
  379.7 5.1 convolution_bitcast_fusion
  384.8 93.0 %all-gather.3.cloned.1.call-done = bf16[8192,512]{0,1:T(8,128)(2,1)} async-done(((bf16[8192,64]{0,1:T(8,128)(2,1)}), bf16[8192,512]{0,1:T(8,128)(2,1)}) %all-gather.3.cloned.1.call-update) | async-done | bytes 8388624 | tf_op jit(solution)/shard_map/all_gather | solution.py:73
  477.8 5.2 fusion.13
  484.1 2.3 reshape.135
  486.4 2.7 copy.17
  489.1 29.9 %all_to_all.15 = bf16[8,2048,64]{1,2,0:T(8,128)(2,1)S(1)} all-to-all(bf16[8,2048,64]{1,2,0:T(8,128)(2,1)S(1)} %copy.17), channel_id=1, replica_groups=mesh['blk'=16,'bal'=8] {'bal'}, dimensions={0} | all-to-all | bytes 4194304 | tf_op jit(solution)/shard_map/all_to_all | solution.py:84
  519.0 2.5 copy.18
  (145 shorter events, 44.0 us)
Async XLA Ops:
  6.5 373.1 %copy-start = (bf16[512,512]{1,0:T(8,128)(2,1)S(1)}, bf16[512,512]{1,0:T(8,128)(2,1)}, u32[]{:S(2)}) copy-start(bf16[512,512]{1,0:T(8,128)(2,1)} %param.18) | copy-start | bytes 1572868
  6.5 3.1 copy-start.3
  6.5 373.1 %all-gather.5.cloned.1.call-start = ((), (), s32[]{:S(2)}) async-start(), calls=%async_computation.2 | async-start | bytes 9437184 | tf_op jit(solution)/shard_map/all_gather | solution.py:74
  7.3 470.5 %all-gather.3.cloned.1.call-start = ((), (), s32[]{:S(2)}) async-start(), calls=%async_computation.1 | async-start | bytes 9437184 | tf_op jit(solution)/shard_map/all_gather | solution.py:73
  7.3 4.7 copy-start.4
  13.3 28.7 %collective-permute-start = (bf16[8192,64]{0,1:T(8,128)(2,1)S(1)}, bf16[8192,64]{0,1:T(8,128)(2,1)}, u32[]{:S(2)}, u32[]{:S(2)}) collective-permute-start(bf16[8192,64]{0,1:T(8,128)(2,1)S(1)} %copy.36), channel_id=1, source_target_pairs={{120,0},{0,8},{8,16},{16,24},{24,32},{32,40},{40,48},{48,56},{56,6... | collective-permute-start | bytes 3145736 | tf_op jit(solution)/shard_map/while/body/eval_jaxpr/ppermute | solution.py:12
  43.2 40.4 %collective-permute-start = (bf16[8192,64]{0,1:T(8,128)(2,1)S(1)}, bf16[8192,64]{0,1:T(8,128)(2,1)}, u32[]{:S(2)}, u32[]{:S(2)}) collective-permute-start(bf16[8192,64]{0,1:T(8,128)(2,1)S(1)} %copy.36), channel_id=1, source_target_pairs={{120,0},{0,8},{8,16},{16,24},{24,32},{32,40},{40,48},{48,56},{56,6... | collective-permute-start | bytes 3145736 | tf_op jit(solution)/shard_map/while/body/eval_jaxpr/ppermute | solution.py:12
  84.8 40.4 %collective-permute-start = (bf16[8192,64]{0,1:T(8,128)(2,1)S(1)}, bf16[8192,64]{0,1:T(8,128)(2,1)}, u32[]{:S(2)}, u32[]{:S(2)}) collective-permute-start(bf16[8192,64]{0,1:T(8,128)(2,1)S(1)} %copy.36), channel_id=1, source_target_pairs={{120,0},{0,8},{8,16},{16,24},{24,32},{32,40},{40,48},{48,56},{56,6... | collective-permute-start | bytes 3145736 | tf_op jit(solution)/shard_map/while/body/eval_jaxpr/ppermute | solution.py:12
  126.4 17.9 %collective-permute-start = (bf16[8192,64]{0,1:T(8,128)(2,1)S(1)}, bf16[8192,64]{0,1:T(8,128)(2,1)}, u32[]{:S(2)}, u32[]{:S(2)}) collective-permute-start(bf16[8192,64]{0,1:T(8,128)(2,1)S(1)} %copy.36), channel_id=1, source_target_pairs={{120,0},{0,8},{8,16},{16,24},{24,32},{32,40},{40,48},{48,56},{56,6... | collective-permute-start | bytes 3145736 | tf_op jit(solution)/shard_map/while/body/eval_jaxpr/ppermute | solution.py:12
  145.5 17.9 %collective-permute-start = (bf16[8192,64]{0,1:T(8,128)(2,1)S(1)}, bf16[8192,64]{0,1:T(8,128)(2,1)}, u32[]{:S(2)}, u32[]{:S(2)}) collective-permute-start(bf16[8192,64]{0,1:T(8,128)(2,1)S(1)} %copy.36), channel_id=1, source_target_pairs={{120,0},{0,8},{8,16},{16,24},{24,32},{32,40},{40,48},{48,56},{56,6... | collective-permute-start | bytes 3145736 | tf_op jit(solution)/shard_map/while/body/eval_jaxpr/ppermute | solution.py:12
  164.7 17.9 %collective-permute-start = (bf16[8192,64]{0,1:T(8,128)(2,1)S(1)}, bf16[8192,64]{0,1:T(8,128)(2,1)}, u32[]{:S(2)}, u32[]{:S(2)}) collective-permute-start(bf16[8192,64]{0,1:T(8,128)(2,1)S(1)} %copy.36), channel_id=1, source_target_pairs={{120,0},{0,8},{8,16},{16,24},{24,32},{32,40},{40,48},{48,56},{56,6... | collective-permute-start | bytes 3145736 | tf_op jit(solution)/shard_map/while/body/eval_jaxpr/ppermute | solution.py:12
  183.9 17.9 %collective-permute-start = (bf16[8192,64]{0,1:T(8,128)(2,1)S(1)}, bf16[8192,64]{0,1:T(8,128)(2,1)}, u32[]{:S(2)}, u32[]{:S(2)}) collective-permute-start(bf16[8192,64]{0,1:T(8,128)(2,1)S(1)} %copy.36), channel_id=1, source_target_pairs={{120,0},{0,8},{8,16},{16,24},{24,32},{32,40},{40,48},{48,56},{56,6... | collective-permute-start | bytes 3145736 | tf_op jit(solution)/shard_map/while/body/eval_jaxpr/ppermute | solution.py:12
  203.0 17.9 %collective-permute-start = (bf16[8192,64]{0,1:T(8,128)(2,1)S(1)}, bf16[8192,64]{0,1:T(8,128)(2,1)}, u32[]{:S(2)}, u32[]{:S(2)}) collective-permute-start(bf16[8192,64]{0,1:T(8,128)(2,1)S(1)} %copy.36), channel_id=1, source_target_pairs={{120,0},{0,8},{8,16},{16,24},{24,32},{32,40},{40,48},{48,56},{56,6... | collective-permute-start | bytes 3145736 | tf_op jit(solution)/shard_map/while/body/eval_jaxpr/ppermute | solution.py:12
  222.2 17.9 %collective-permute-start = (bf16[8192,64]{0,1:T(8,128)(2,1)S(1)}, bf16[8192,64]{0,1:T(8,128)(2,1)}, u32[]{:S(2)}, u32[]{:S(2)}) collective-permute-start(bf16[8192,64]{0,1:T(8,128)(2,1)S(1)} %copy.36), channel_id=1, source_target_pairs={{120,0},{0,8},{8,16},{16,24},{24,32},{32,40},{40,48},{48,56},{56,6... | collective-permute-start | bytes 3145736 | tf_op jit(solution)/shard_map/while/body/eval_jaxpr/ppermute | solution.py:12
  241.4 17.9 %collective-permute-start = (bf16[8192,64]{0,1:T(8,128)(2,1)S(1)}, bf16[8192,64]{0,1:T(8,128)(2,1)}, u32[]{:S(2)}, u32[]{:S(2)}) collective-permute-start(bf16[8192,64]{0,1:T(8,128)(2,1)S(1)} %copy.36), channel_id=1, source_target_pairs={{120,0},{0,8},{8,16},{16,24},{24,32},{32,40},{40,48},{48,56},{56,6... | collective-permute-start | bytes 3145736 | tf_op jit(solution)/shard_map/while/body/eval_jaxpr/ppermute | solution.py:12
  260.6 17.9 %collective-permute-start = (bf16[8192,64]{0,1:T(8,128)(2,1)S(1)}, bf16[8192,64]{0,1:T(8,128)(2,1)}, u32[]{:S(2)}, u32[]{:S(2)}) collective-permute-start(bf16[8192,64]{0,1:T(8,128)(2,1)S(1)} %copy.36), channel_id=1, source_target_pairs={{120,0},{0,8},{8,16},{16,24},{24,32},{32,40},{40,48},{48,56},{56,6... | collective-permute-start | bytes 3145736 | tf_op jit(solution)/shard_map/while/body/eval_jaxpr/ppermute | solution.py:12
  279.7 17.9 %collective-permute-start = (bf16[8192,64]{0,1:T(8,128)(2,1)S(1)}, bf16[8192,64]{0,1:T(8,128)(2,1)}, u32[]{:S(2)}, u32[]{:S(2)}) collective-permute-start(bf16[8192,64]{0,1:T(8,128)(2,1)S(1)} %copy.36), channel_id=1, source_target_pairs={{120,0},{0,8},{8,16},{16,24},{24,32},{32,40},{40,48},{48,56},{56,6... | collective-permute-start | bytes 3145736 | tf_op jit(solution)/shard_map/while/body/eval_jaxpr/ppermute | solution.py:12
  298.9 17.9 %collective-permute-start = (bf16[8192,64]{0,1:T(8,128)(2,1)S(1)}, bf16[8192,64]{0,1:T(8,128)(2,1)}, u32[]{:S(2)}, u32[]{:S(2)}) collective-permute-start(bf16[8192,64]{0,1:T(8,128)(2,1)S(1)} %copy.36), channel_id=1, source_target_pairs={{120,0},{0,8},{8,16},{16,24},{24,32},{32,40},{40,48},{48,56},{56,6... | collective-permute-start | bytes 3145736 | tf_op jit(solution)/shard_map/while/body/eval_jaxpr/ppermute | solution.py:12
  318.1 17.9 %collective-permute-start = (bf16[8192,64]{0,1:T(8,128)(2,1)S(1)}, bf16[8192,64]{0,1:T(8,128)(2,1)}, u32[]{:S(2)}, u32[]{:S(2)}) collective-permute-start(bf16[8192,64]{0,1:T(8,128)(2,1)S(1)} %copy.36), channel_id=1, source_target_pairs={{120,0},{0,8},{8,16},{16,24},{24,32},{32,40},{40,48},{48,56},{56,6... | collective-permute-start | bytes 3145736 | tf_op jit(solution)/shard_map/while/body/eval_jaxpr/ppermute | solution.py:12
  337.2 17.9 %collective-permute-start = (bf16[8192,64]{0,1:T(8,128)(2,1)S(1)}, bf16[8192,64]{0,1:T(8,128)(2,1)}, u32[]{:S(2)}, u32[]{:S(2)}) collective-permute-start(bf16[8192,64]{0,1:T(8,128)(2,1)S(1)} %copy.36), channel_id=1, source_target_pairs={{120,0},{0,8},{8,16},{16,24},{24,32},{32,40},{40,48},{48,56},{56,6... | collective-permute-start | bytes 3145736 | tf_op jit(solution)/shard_map/while/body/eval_jaxpr/ppermute | solution.py:12
  357.7 5.2 copy-start.1
  377.4 1.2 copy-start.2
Sparse Core Ops, SparseCore 0:
  9.0 94.5 all-gather.4
  378.6 99.1 all-gather.2
where the time goes:
time: 533 us; the launch traced here: 528 us
  waiting for transfers between devices  290 us (54%)
  other arithmetic  88.5 us (17%)
  matrix products  56 us (11%)
  local copies, waits for them, and re-layouts  49.7 us (9%)
  blocking collectives  29.9 us (6%)
  between operations  13.5 us (3%)
    ppermute x15, waiting for transfers between devices, from_behind(): return lax.ppermute(block, axis, route)  196 us
    all_gather x1, waiting for transfers between devices, on_device(): mean_piece = lax.all_gather(mean_agg, 'bal', axis=1, tiled=True)  93 us
    scatter-add x16, other arithmetic, absorb(): return total.at[targets].add(masked)  75.5 us
    dot_general x16, matrix products, absorb(): jnp.einsum('sij,sjf->sif', vals, gathered, preferred_element_type=jnp.flo...  34.2 us
    all_to_all x1, blocking collectives, on_device(): lax.all_to_all(placed.astype(jnp.bfloat16).reshape(n_bal, capacity * TILE...  29.9 us
    another operation x15, local copies, waits for them, and re-layouts  18.4 us
    gather x16, local copies, waits for them, and re-layouts, absorb(): gathered = jnp.take(tiles, picks, axis=0)  11.8 us
    and x16, other arithmetic, absorb(): gathered = jnp.take(tiles, picks, axis=0)  11.2 us
  transfers between devices with their start and end apart: 17, of which 16 were waited for; matrix products, arithmetic and copies ran while one was open for 34% of the time, Pallas kernels for 0%

commit v1 on v0

--- a/solution.py
+++ b/solution.py
@@ -2,6 +2,7 @@
 import jax.numpy as jnp
 from jax import lax
 from jax.sharding import PartitionSpec as P
+from jax.lax import all_gather
 
 TILE = 128
 
@@ -70,8 +71,11 @@
     col_start = column * width
     zeros_out = jnp.zeros((tiles_per * TILE, width), jnp.float32)
     carry = zeros_out
-    mean_piece = lax.all_gather(mean_agg, "bal", axis=1, tiled=True)
-    feat_piece = lax.all_gather(features, "bal", axis=1, tiled=True)
+    mean_piece, feat_piece = jnp.split(
+        all_gather(jnp.concatenate([mean_agg, features], 0), axis=1, tiled=True, axis_name="bal"),
+        [mean_agg.shape[0]],
+        0,
+    )
     count = mean_piece.shape[1]
     neigh_part = lax.dynamic_slice(w_neigh, (0, col_start), (count, width))
     self_part = lax.dynamic_slice(w_self, (0, col_start), (count, width))

time: 533 us -> 556 us (1.043)
  waiting for transfers between devices: 290 us -> 310 us
    all_gather x2 -> x1, waiting for transfers between devices: 93.1 us -> 169 us  [on_device(): all_gather(jnp.concatenate([mean_agg, features], 0), axis=1, tiled=True,...]
    ppermute x15, waiting for transfers between devices: 196 us -> 141 us  [from_behind(): return lax.ppermute(block, axis, route)]
  transfers between devices with their start and end apart: 17 -> 16, of which waited for: 16 -> 16; matrix products, arithmetic and copies ran while one was open for 34% -> 23% of each run, Pallas kernels for 0% -> 0%
where the time goes in v1:
time: 556 us; the launch traced here: 551 us
  waiting for transfers between devices  310 us (56%)
  other arithmetic  89.6 us (16%)
  matrix products  56 us (10%)
  local copies, waits for them, and re-layouts  51.4 us (9%)
  blocking collectives  29.9 us (5%)
  between operations  13.5 us (2%)
    all_gather x1, waiting for transfers between devices, on_device(): all_gather(jnp.concatenate([mean_agg, features], 0), axis=1, tiled=True,...  169 us
    ppermute x15, waiting for transfers between devices, from_behind(): return lax.ppermute(block, axis, route)  141 us
    scatter-add x16, other arithmetic, absorb(): return total.at[targets].add(masked)  75.4 us
    dot_general x16, matrix products, absorb(): jnp.einsum('sij,sjf->sif', vals, gathered, preferred_element_type=jnp.flo...  34.1 us
    all_to_all x1, blocking collectives, on_device(): lax.all_to_all(placed.astype(jnp.bfloat16).reshape(n_bal, capacity * TILE...  29.9 us
    another operation x15, local copies, waits for them, and re-layouts  18.4 us
    gather x16, local copies, waits for them, and re-layouts, absorb(): gathered = jnp.take(tiles, picks, axis=0)  11.8 us
    and x16, other arithmetic, absorb(): gathered = jnp.take(tiles, picks, axis=0)  11.2 us
  transfers between devices with their start and end apart: 16, of which 16 were waited for; matrix products, arithmetic and copies ran while one was open for 23% of the time, Pallas kernels for 0%

profile of v1, /device:TPU:0, one launch (start us, length us, event | category | flops | bytes accessed | tf_op | source)
XLA Modules:
  0.0 550.8 jit_solution(15338272817525731059)
XLA Ops:
  8.0 2.3 copy.33
  10.4 10.2 %fusion.43 = f32[1,16,32,128]{3,0,2,1:T(1,128)S(1)} fusion(bf16[1,16,32,128,128]{4,3,2,1,0:T(8,128)(2,1)} %param.14), kind=kOutput, calls=%fused_computation.73 | convolution fusion | flops 16777216 | bytes 17039360 | tf_op jit(solution)/shard_map/csij,j->csi/dot_general | solution.py:38
  20.5 1.6 broadcast_in_dim.81
  22.1 287.5 %while.17 = (s32[]{:T(128)}, f32[64,128,64]{1,2,0:T(8,128)}, bf16[8192,64]{0,1:T(8,128)(2,1)}, s32[]{:T(128)}, s32[16,32]{1,0:T(8,128)S(1)}, /*index=5*/pred[16,...) while((s32[]{:T(128)}, f32[64,128,64]{1,2,0:T(8,128)}, ...), condition=%wide.region_4.6_spmd, body=%wide.region_2.5_spmd.sunk | while | flops 67896624 | bytes 15209832 | solution.py:62
  25.1 2.1 convolution_select_fusion.3
  27.1 4.8 scatter_fusion
  31.9 9.4 %collective-permute-done = bf16[8192,64]{0,1:T(8,128)(2,1)} collective-permute-done((bf16[8192,64]{0,1:T(8,128)(2,1)S(1)}, bf16[8192,64]{0,1:T(8,128)(2,1)}, u32[]{:S(2)}, u32[]{:S(2)}) %collective-permute-start) | collective-permute-done | bytes 1048608 | tf_op jit(solution)/shard_map/while/body/eval_jaxpr/ppermute | solution.py:13
  44.2 2.1 convolution_select_fusion.3
  46.3 4.8 scatter_fusion
  51.1 9.4 %collective-permute-done = bf16[8192,64]{0,1:T(8,128)(2,1)} collective-permute-done((bf16[8192,64]{0,1:T(8,128)(2,1)S(1)}, bf16[8192,64]{0,1:T(8,128)(2,1)}, u32[]{:S(2)}, u32[]{:S(2)}) %collective-permute-start) | collective-permute-done | bytes 1048608 | tf_op jit(solution)/shard_map/while/body/eval_jaxpr/ppermute | solution.py:13
  63.4 2.1 convolution_select_fusion.3
  65.5 4.8 scatter_fusion
  70.3 9.4 %collective-permute-done = bf16[8192,64]{0,1:T(8,128)(2,1)} collective-permute-done((bf16[8192,64]{0,1:T(8,128)(2,1)S(1)}, bf16[8192,64]{0,1:T(8,128)(2,1)}, u32[]{:S(2)}, u32[]{:S(2)}) %collective-permute-start) | collective-permute-done | bytes 1048608 | tf_op jit(solution)/shard_map/while/body/eval_jaxpr/ppermute | solution.py:13
  79.6 1.2 copy.36
  82.6 2.1 convolution_select_fusion.3
  84.6 4.8 scatter_fusion
  89.4 9.4 %collective-permute-done = bf16[8192,64]{0,1:T(8,128)(2,1)} collective-permute-done((bf16[8192,64]{0,1:T(8,128)(2,1)S(1)}, bf16[8192,64]{0,1:T(8,128)(2,1)}, u32[]{:S(2)}, u32[]{:S(2)}) %collective-permute-start) | collective-permute-done | bytes 1048608 | tf_op jit(solution)/shard_map/while/body/eval_jaxpr/ppermute | solution.py:13
  101.7 2.1 convolution_select_fusion.3
  103.8 4.8 scatter_fusion
  108.6 9.4 %collective-permute-done = bf16[8192,64]{0,1:T(8,128)(2,1)} collective-permute-done((bf16[8192,64]{0,1:T(8,128)(2,1)S(1)}, bf16[8192,64]{0,1:T(8,128)(2,1)}, u32[]{:S(2)}, u32[]{:S(2)}) %collective-permute-start) | collective-permute-done | bytes 1048608 | tf_op jit(solution)/shard_map/while/body/eval_jaxpr/ppermute | solution.py:13
  120.9 2.1 convolution_select_fusion.3
  123.0 4.8 scatter_fusion
  127.8 9.4 %collective-permute-done = bf16[8192,64]{0,1:T(8,128)(2,1)} collective-permute-done((bf16[8192,64]{0,1:T(8,128)(2,1)S(1)}, bf16[8192,64]{0,1:T(8,128)(2,1)}, u32[]{:S(2)}, u32[]{:S(2)}) %collective-permute-start) | collective-permute-done | bytes 1048608 | tf_op jit(solution)/shard_map/while/body/eval_jaxpr/ppermute | solution.py:13
  137.2 1.2 copy.36
  140.1 2.1 convolution_select_fusion.3
  142.2 4.8 scatter_fusion
  146.9 9.4 %collective-permute-done = bf16[8192,64]{0,1:T(8,128)(2,1)} collective-permute-done((bf16[8192,64]{0,1:T(8,128)(2,1)S(1)}, bf16[8192,64]{0,1:T(8,128)(2,1)}, u32[]{:S(2)}, u32[]{:S(2)}) %collective-permute-start) | collective-permute-done | bytes 1048608 | tf_op jit(solution)/shard_map/while/body/eval_jaxpr/ppermute | solution.py:13
  159.2 2.1 convolution_select_fusion.3
  161.3 4.8 scatter_fusion
  166.1 9.4 %collective-permute-done = bf16[8192,64]{0,1:T(8,128)(2,1)} collective-permute-done((bf16[8192,64]{0,1:T(8,128)(2,1)S(1)}, bf16[8192,64]{0,1:T(8,128)(2,1)}, u32[]{:S(2)}, u32[]{:S(2)}) %collective-permute-start) | collective-permute-done | bytes 1048608 | tf_op jit(solution)/shard_map/while/body/eval_jaxpr/ppermute | solution.py:13
  178.4 2.1 convolution_select_fusion.3
  180.5 4.8 scatter_fusion
  185.3 9.4 %collective-permute-done = bf16[8192,64]{0,1:T(8,128)(2,1)} collective-permute-done((bf16[8192,64]{0,1:T(8,128)(2,1)S(1)}, bf16[8192,64]{0,1:T(8,128)(2,1)}, u32[]{:S(2)}, u32[]{:S(2)}) %collective-permute-start) | collective-permute-done | bytes 1048608 | tf_op jit(solution)/shard_map/while/body/eval_jaxpr/ppermute | solution.py:13
  194.7 1.2 copy.36
  197.6 2.1 convolution_select_fusion.3
  199.7 4.8 scatter_fusion
  204.4 9.4 %collective-permute-done = bf16[8192,64]{0,1:T(8,128)(2,1)} collective-permute-done((bf16[8192,64]{0,1:T(8,128)(2,1)S(1)}, bf16[8192,64]{0,1:T(8,128)(2,1)}, u32[]{:S(2)}, u32[]{:S(2)}) %collective-permute-start) | collective-permute-done | bytes 1048608 | tf_op jit(solution)/shard_map/while/body/eval_jaxpr/ppermute | solution.py:13
  216.8 2.1 convolution_select_fusion.3
  218.8 4.8 scatter_fusion
  223.6 9.4 %collective-permute-done = bf16[8192,64]{0,1:T(8,128)(2,1)} collective-permute-done((bf16[8192,64]{0,1:T(8,128)(2,1)S(1)}, bf16[8192,64]{0,1:T(8,128)(2,1)}, u32[]{:S(2)}, u32[]{:S(2)}) %collective-permute-start) | collective-permute-done | bytes 1048608 | tf_op jit(solution)/shard_map/while/body/eval_jaxpr/ppermute | solution.py:13
  235.9 2.1 convolution_select_fusion.3
  238.0 4.8 scatter_fusion
  242.8 9.4 %collective-permute-done = bf16[8192,64]{0,1:T(8,128)(2,1)} collective-permute-done((bf16[8192,64]{0,1:T(8,128)(2,1)S(1)}, bf16[8192,64]{0,1:T(8,128)(2,1)}, u32[]{:S(2)}, u32[]{:S(2)}) %collective-permute-start) | collective-permute-done | bytes 1048608 | tf_op jit(solution)/shard_map/while/body/eval_jaxpr/ppermute | solution.py:13
  255.1 2.1 convolution_select_fusion.3
  257.2 4.8 scatter_fusion
  261.9 9.4 %collective-permute-done = bf16[8192,64]{0,1:T(8,128)(2,1)} collective-permute-done((bf16[8192,64]{0,1:T(8,128)(2,1)S(1)}, bf16[8192,64]{0,1:T(8,128)(2,1)}, u32[]{:S(2)}, u32[]{:S(2)}) %collective-permute-start) | collective-permute-done | bytes 1048608 | tf_op jit(solution)/shard_map/while/body/eval_jaxpr/ppermute | solution.py:13
  274.3 2.1 convolution_select_fusion.3
  276.3 4.8 scatter_fusion
  281.1 9.4 %collective-permute-done = bf16[8192,64]{0,1:T(8,128)(2,1)} collective-permute-done((bf16[8192,64]{0,1:T(8,128)(2,1)S(1)}, bf16[8192,64]{0,1:T(8,128)(2,1)}, u32[]{:S(2)}, u32[]{:S(2)}) %collective-permute-start) | collective-permute-done | bytes 1048608 | tf_op jit(solution)/shard_map/while/body/eval_jaxpr/ppermute | solution.py:13
  293.4 2.1 convolution_select_fusion.3
  295.5 4.8 scatter_fusion
  300.3 9.4 %collective-permute-done = bf16[8192,64]{0,1:T(8,128)(2,1)} collective-permute-done((bf16[8192,64]{0,1:T(8,128)(2,1)S(1)}, bf16[8192,64]{0,1:T(8,128)(2,1)}, u32[]{:S(2)}, u32[]{:S(2)}) %collective-permute-start) | collective-permute-done | bytes 1048608 | tf_op jit(solution)/shard_map/while/body/eval_jaxpr/ppermute | solution.py:13
  309.7 2.6 copy_bitcast_fusion.2
  312.8 2.0 gather_fusion.1
  314.8 3.1 convolution_select_fusion.1
  317.9 3.8 scatter_fusion.1
  322.9 1.5 pad_maximum_fusion
  326.1 169.0 %all-gather.2.cloned.1.call-done = bf16[16384,512]{0,1:T(8,128)(2,1)} async-done(((bf16[16384,64]{0,1:T(8,128)(2,1)}), bf16[16384,512]{0,1:T(8,128)(2,1)}) %all-gather.2.cloned.1.call-update) | async-done | bytes 16777232 | tf_op jit(solution)/shard_map/all_gather | solution.py:75
  495.1 5.1 fusion.14
  500.2 5.2 fusion.16
  506.5 2.3 reshape.135
  508.8 2.7 copy.17
  511.5 29.9 %all_to_all.15 = bf16[8,2048,64]{1,2,0:T(8,128)(2,1)S(1)} all-to-all(bf16[8,2048,64]{1,2,0:T(8,128)(2,1)S(1)} %copy.17), channel_id=1, replica_groups=mesh['blk'=16,'bal'=8] {'bal'}, dimensions={0} | all-to-all | bytes 4194304 | tf_op jit(solution)/shard_map/all_to_all | solution.py:88
  541.4 2.5 copy.18
  (143 shorter events, 45.9 us)
Async XLA Ops:
  6.5 488.5 %copy-start = (bf16[512,512]{1,0:T(8,128)(2,1)S(1)}, bf16[512,512]{1,0:T(8,128)(2,1)}, u32[]{:S(2)}) copy-start(bf16[512,512]{1,0:T(8,128)(2,1)} %param.19) | copy-start | bytes 1572868
  6.5 3.8 copy-start.4
  6.5 488.5 %all-gather.2.cloned.1.call-start = ((), (), s32[]{:S(2)}) async-start(), calls=%async_computation.1 | async-start | bytes 18874368 | tf_op jit(solution)/shard_map/all_gather | solution.py:75
  23.4 17.9 %collective-permute-start = (bf16[8192,64]{0,1:T(8,128)(2,1)S(1)}, bf16[8192,64]{0,1:T(8,128)(2,1)}, u32[]{:S(2)}, u32[]{:S(2)}) collective-permute-start(bf16[8192,64]{0,1:T(8,128)(2,1)S(1)} %copy.36), channel_id=1, source_target_pairs={{120,0},{0,8},{8,16},{16,24},{24,32},{32,40},{40,48},{48,56},{56,6... | collective-permute-start | bytes 3145736 | tf_op jit(solution)/shard_map/while/body/eval_jaxpr/ppermute | solution.py:13
  42.5 17.9 %collective-permute-start = (bf16[8192,64]{0,1:T(8,128)(2,1)S(1)}, bf16[8192,64]{0,1:T(8,128)(2,1)}, u32[]{:S(2)}, u32[]{:S(2)}) collective-permute-start(bf16[8192,64]{0,1:T(8,128)(2,1)S(1)} %copy.36), channel_id=1, source_target_pairs={{120,0},{0,8},{8,16},{16,24},{24,32},{32,40},{40,48},{48,56},{56,6... | collective-permute-start | bytes 3145736 | tf_op jit(solution)/shard_map/while/body/eval_jaxpr/ppermute | solution.py:13
  61.7 17.9 %collective-permute-start = (bf16[8192,64]{0,1:T(8,128)(2,1)S(1)}, bf16[8192,64]{0,1:T(8,128)(2,1)}, u32[]{:S(2)}, u32[]{:S(2)}) collective-permute-start(bf16[8192,64]{0,1:T(8,128)(2,1)S(1)} %copy.36), channel_id=1, source_target_pairs={{120,0},{0,8},{8,16},{16,24},{24,32},{32,40},{40,48},{48,56},{56,6... | collective-permute-start | bytes 3145736 | tf_op jit(solution)/shard_map/while/body/eval_jaxpr/ppermute | solution.py:13
  80.9 17.9 %collective-permute-start = (bf16[8192,64]{0,1:T(8,128)(2,1)S(1)}, bf16[8192,64]{0,1:T(8,128)(2,1)}, u32[]{:S(2)}, u32[]{:S(2)}) collective-permute-start(bf16[8192,64]{0,1:T(8,128)(2,1)S(1)} %copy.36), channel_id=1, source_target_pairs={{120,0},{0,8},{8,16},{16,24},{24,32},{32,40},{40,48},{48,56},{56,6... | collective-permute-start | bytes 3145736 | tf_op jit(solution)/shard_map/while/body/eval_jaxpr/ppermute | solution.py:13
  100.0 17.9 %collective-permute-start = (bf16[8192,64]{0,1:T(8,128)(2,1)S(1)}, bf16[8192,64]{0,1:T(8,128)(2,1)}, u32[]{:S(2)}, u32[]{:S(2)}) collective-permute-start(bf16[8192,64]{0,1:T(8,128)(2,1)S(1)} %copy.36), channel_id=1, source_target_pairs={{120,0},{0,8},{8,16},{16,24},{24,32},{32,40},{40,48},{48,56},{56,6... | collective-permute-start | bytes 3145736 | tf_op jit(solution)/shard_map/while/body/eval_jaxpr/ppermute | solution.py:13
  119.2 17.9 %collective-permute-start = (bf16[8192,64]{0,1:T(8,128)(2,1)S(1)}, bf16[8192,64]{0,1:T(8,128)(2,1)}, u32[]{:S(2)}, u32[]{:S(2)}) collective-permute-start(bf16[8192,64]{0,1:T(8,128)(2,1)S(1)} %copy.36), channel_id=1, source_target_pairs={{120,0},{0,8},{8,16},{16,24},{24,32},{32,40},{40,48},{48,56},{56,6... | collective-permute-start | bytes 3145736 | tf_op jit(solution)/shard_map/while/body/eval_jaxpr/ppermute | solution.py:13
  138.4 17.9 %collective-permute-start = (bf16[8192,64]{0,1:T(8,128)(2,1)S(1)}, bf16[8192,64]{0,1:T(8,128)(2,1)}, u32[]{:S(2)}, u32[]{:S(2)}) collective-permute-start(bf16[8192,64]{0,1:T(8,128)(2,1)S(1)} %copy.36), channel_id=1, source_target_pairs={{120,0},{0,8},{8,16},{16,24},{24,32},{32,40},{40,48},{48,56},{56,6... | collective-permute-start | bytes 3145736 | tf_op jit(solution)/shard_map/while/body/eval_jaxpr/ppermute | solution.py:13
  157.5 17.9 %collective-permute-start = (bf16[8192,64]{0,1:T(8,128)(2,1)S(1)}, bf16[8192,64]{0,1:T(8,128)(2,1)}, u32[]{:S(2)}, u32[]{:S(2)}) collective-permute-start(bf16[8192,64]{0,1:T(8,128)(2,1)S(1)} %copy.36), channel_id=1, source_target_pairs={{120,0},{0,8},{8,16},{16,24},{24,32},{32,40},{40,48},{48,56},{56,6... | collective-permute-start | bytes 3145736 | tf_op jit(solution)/shard_map/while/body/eval_jaxpr/ppermute | solution.py:13
  176.7 17.9 %collective-permute-start = (bf16[8192,64]{0,1:T(8,128)(2,1)S(1)}, bf16[8192,64]{0,1:T(8,128)(2,1)}, u32[]{:S(2)}, u32[]{:S(2)}) collective-permute-start(bf16[8192,64]{0,1:T(8,128)(2,1)S(1)} %copy.36), channel_id=1, source_target_pairs={{120,0},{0,8},{8,16},{16,24},{24,32},{32,40},{40,48},{48,56},{56,6... | collective-permute-start | bytes 3145736 | tf_op jit(solution)/shard_map/while/body/eval_jaxpr/ppermute | solution.py:13
  195.9 17.9 %collective-permute-start = (bf16[8192,64]{0,1:T(8,128)(2,1)S(1)}, bf16[8192,64]{0,1:T(8,128)(2,1)}, u32[]{:S(2)}, u32[]{:S(2)}) collective-permute-start(bf16[8192,64]{0,1:T(8,128)(2,1)S(1)} %copy.36), channel_id=1, source_target_pairs={{120,0},{0,8},{8,16},{16,24},{24,32},{32,40},{40,48},{48,56},{56,6... | collective-permute-start | bytes 3145736 | tf_op jit(solution)/shard_map/while/body/eval_jaxpr/ppermute | solution.py:13
  215.1 17.9 %collective-permute-start = (bf16[8192,64]{0,1:T(8,128)(2,1)S(1)}, bf16[8192,64]{0,1:T(8,128)(2,1)}, u32[]{:S(2)}, u32[]{:S(2)}) collective-permute-start(bf16[8192,64]{0,1:T(8,128)(2,1)S(1)} %copy.36), channel_id=1, source_target_pairs={{120,0},{0,8},{8,16},{16,24},{24,32},{32,40},{40,48},{48,56},{56,6... | collective-permute-start | bytes 3145736 | tf_op jit(solution)/shard_map/while/body/eval_jaxpr/ppermute | solution.py:13
  234.2 17.9 %collective-permute-start = (bf16[8192,64]{0,1:T(8,128)(2,1)S(1)}, bf16[8192,64]{0,1:T(8,128)(2,1)}, u32[]{:S(2)}, u32[]{:S(2)}) collective-permute-start(bf16[8192,64]{0,1:T(8,128)(2,1)S(1)} %copy.36), channel_id=1, source_target_pairs={{120,0},{0,8},{8,16},{16,24},{24,32},{32,40},{40,48},{48,56},{56,6... | collective-permute-start | bytes 3145736 | tf_op jit(solution)/shard_map/while/body/eval_jaxpr/ppermute | solution.py:13
  253.4 17.9 %collective-permute-start = (bf16[8192,64]{0,1:T(8,128)(2,1)S(1)}, bf16[8192,64]{0,1:T(8,128)(2,1)}, u32[]{:S(2)}, u32[]{:S(2)}) collective-permute-start(bf16[8192,64]{0,1:T(8,128)(2,1)S(1)} %copy.36), channel_id=1, source_target_pairs={{120,0},{0,8},{8,16},{16,24},{24,32},{32,40},{40,48},{48,56},{56,6... | collective-permute-start | bytes 3145736 | tf_op jit(solution)/shard_map/while/body/eval_jaxpr/ppermute | solution.py:13
  272.6 17.9 %collective-permute-start = (bf16[8192,64]{0,1:T(8,128)(2,1)S(1)}, bf16[8192,64]{0,1:T(8,128)(2,1)}, u32[]{:S(2)}, u32[]{:S(2)}) collective-permute-start(bf16[8192,64]{0,1:T(8,128)(2,1)S(1)} %copy.36), channel_id=1, source_target_pairs={{120,0},{0,8},{8,16},{16,24},{24,32},{32,40},{40,48},{48,56},{56,6... | collective-permute-start | bytes 3145736 | tf_op jit(solution)/shard_map/while/body/eval_jaxpr/ppermute | solution.py:13
  291.7 17.9 %collective-permute-start = (bf16[8192,64]{0,1:T(8,128)(2,1)S(1)}, bf16[8192,64]{0,1:T(8,128)(2,1)}, u32[]{:S(2)}, u32[]{:S(2)}) collective-permute-start(bf16[8192,64]{0,1:T(8,128)(2,1)S(1)} %copy.36), channel_id=1, source_target_pairs={{120,0},{0,8},{8,16},{16,24},{24,32},{32,40},{40,48},{48,56},{56,6... | collective-permute-start | bytes 3145736 | tf_op jit(solution)/shard_map/while/body/eval_jaxpr/ppermute | solution.py:13
  312.8 5.1 copy-start.1
  321.6 1.2 copy-start.2
  324.3 0.7 copy-start.3
Sparse Core Ops, SparseCore 0:
  324.5 170.5 all-gather.1
